TPU v7x, 256 devices: a whole 4x4x8 slice. The times are simulated.
256 devices in a mesh: dp: 32 (over z, x), mp: 8 (over y, core).
Axes of the slice: x: 4, y: 4, z: 8, core: 2. Of those that a mesh axis runs over, the one named last changes fastest.
Arguments:
- tokens: bfloat16 [32768, 8192], P('dp', 'mp'), may hold values from -6 to 6
- value_weight: bfloat16 [8192, 1024], P('mp'), may hold values from -0.0625 to 0.0625
- adapter_down_panels: bfloat16 [96, 64, 8192], P('dp', None, 'mp'), may hold values from -0.0625 to 0.0625
- adapter_up_panels: bfloat16 [96, 64, 1024], P('dp', None, 'mp'), may hold values from -0.75 to 0.75
- cotangent: bfloat16 [32768, 1024], P('dp', 'mp'), may hold values from -6 to 6
- block_list_entry: int32 [1024], P('dp'), may hold values from 0 to 31, as said below
- device_tenant_list: int32 [1024], P('dp'), may hold values from 0 to 95, as said below
- tenant_location_map: int32 [96], replicated, may hold values from 0 to 95, as said below
Outputs:
- values: bfloat16 [32768, 1024], P('dp', 'mp')
- token_gradient: bfloat16 [32768, 8192], P('dp', 'mp')
- grad_a: bfloat16 [96, 64, 8192], P('dp', None, 'mp')
- grad_b: bfloat16 [96, 64, 1024], P('dp', None, 'mp')
Inputs may be any that keep to these rules, and one draw needn't show every extreme that they name: `device_tenant_list`: each entry names a tenant; no tenant stands twice in one list. Of one device's 32 entries, at most 2 name tenants whose storage location tenant_location_map[t] lies on one dp index (tenant_location_map[t] // 3), and every device's list has 2 entries on some one dp index. A permutation: tenant t's panels are row tenant_location_map[t] of adapter_down_panels and adapter_up_panels. `block_list_entry`: every entry of a device's tenant list is named by at least one of that device's row blocks.
All inputs are finite; a program needn't handle non-finite values.
Results may differ from a plain program's by a relative error of at most 0.0057.
Values may be sent and summed in bfloat16 or wider, within the bound.
A program may use at most 128 MiB of HBM per device.

v0:
```python
import jax
import jax.numpy as jnp
from jax import lax
from jax.sharding import PartitionSpec as P

MOST = 2


def compare_table(left, right):
    return left[:, None] == right[None, :]


def shards(
    tokens,
    value_weight,
    adapter_down_panels,
    adapter_up_panels,
    cotangent,
    block_list_entry,
    device_tenant_list,
    tenant_location_map,
):
    rows, width_loc = tokens.shape
    stored_panels, adapter_rank_size, ignored_result = adapter_down_panels.shape
    output_location = adapter_up_panels.shape[2]
    blocks = block_list_entry.shape[0]
    block_rows = rows // blocks
    listed = device_tenant_list.shape[0]
    tenants = tenant_location_map.shape[0]
    capacity = lax.axis_size("dp") * MOST
    slot_ids = jnp.arange(listed, dtype=jnp.int32)
    tenant_ids = jnp.arange(tenants, dtype=jnp.int32)
    storage_location = jnp.sum(
        jnp.where(compare_table(device_tenant_list, tenant_ids), tenant_location_map[None, :], 0),
        axis=1,
    )
    holder = storage_location // stored_panels
    local_row = storage_location % stored_panels
    earlier = slot_ids[:, None] > slot_ids[None, :]
    rank_at = jnp.sum(jnp.where(compare_table(holder, holder) & earlier, 1, 0), axis=1).astype(
        jnp.int32
    )
    position = holder * MOST + rank_at
    canonical = jnp.min(
        jnp.where(compare_table(device_tenant_list, device_tenant_list), slot_ids[None, :], listed),
        axis=1,
    )
    block_canon = jnp.sum(
        jnp.where(compare_table(block_list_entry, slot_ids), canonical[None, :], 0), axis=1
    )
    requests = jnp.zeros((capacity,), jnp.int32).at[position].set(local_row + 1)
    incoming = lax.all_to_all(requests, "dp", split_axis=0, concat_axis=0, tiled=True)
    serve_adapters = compare_table(
        incoming, jnp.arange(1, stored_panels + 1, dtype=jnp.int32)
    ).astype(jnp.bfloat16)
    returned_down_panel = jnp.einsum(
        "vj,jiz->viz", serve_adapters, adapter_down_panels, preferred_element_type=jnp.float32
    ).astype(jnp.bfloat16)
    returned_up_panel = jnp.einsum(
        "wu,une->wne", serve_adapters, adapter_up_panels, preferred_element_type=jnp.float32
    ).astype(jnp.bfloat16)
    got_a, got_b = (
        lax.all_to_all(returned_down_panel, "dp", split_axis=0, concat_axis=0, tiled=True),
        lax.all_to_all(returned_up_panel, "dp", split_axis=0, concat_axis=0, tiled=True),
    )
    slot_a = got_a[position]
    slot_b = got_b[position]
    w_cols = value_weight
    base_flipped_weight = lax.psum_scatter(
        lax.dot_general(
            w_cols, tokens, (((0,), (1,)), ((), ())), preferred_element_type=jnp.float32
        ),
        "mp",
        scatter_dimension=0,
        tiled=True,
    )
    token_blocks = tokens.reshape(blocks, block_rows, width_loc)
    cot_blocks = cotangent.reshape(blocks, block_rows, output_location)
    block_down_panel = slot_a[block_list_entry]
    block_up_panel = slot_b[block_list_entry]
    down_part = jnp.einsum(
        "bnd,brd->bnr", token_blocks, block_down_panel, preferred_element_type=jnp.float32
    )
    down_low = lax.psum(down_part, "mp").astype(jnp.bfloat16)
    adapter_output = jnp.einsum(
        "afq,aqy->afy", down_low, block_up_panel, preferred_element_type=jnp.float32
    ).reshape(rows, output_location)
    values = (base_flipped_weight.T + adapter_output).astype(jnp.bfloat16)
    up_part = jnp.einsum(
        "bnc,brc->bnr", cot_blocks, block_up_panel, preferred_element_type=jnp.float32
    )
    up_grad = lax.psum(up_part, "mp").astype(jnp.bfloat16)
    w_cols = value_weight
    base_backward_pass = lax.dot_general(
        lax.all_gather(cotangent, "mp", axis=1, tiled=True),
        w_cols,
        (((1,), (1,)), ((), ())),
        preferred_element_type=jnp.float32,
    )
    adapter_backward_pass = jnp.einsum(
        "swq,sqj->swj", up_grad, block_down_panel, preferred_element_type=jnp.float32
    ).reshape(rows, width_loc)
    token_gradient = (base_backward_pass + adapter_backward_pass).astype(jnp.bfloat16)
    block_grad_a = jnp.einsum(
        "bnr,bnd->brd", up_grad, token_blocks, preferred_element_type=jnp.float32
    )
    block_grad_b = jnp.einsum(
        "bnr,bnc->brc", down_low, cot_blocks, preferred_element_type=jnp.float32
    )
    gather_slots = compare_table(block_canon, slot_ids).astype(jnp.float32)
    share_a = jnp.einsum(
        "bs,brd->srd", gather_slots, block_grad_a, precision=lax.Precision.HIGHEST
    ).astype(jnp.bfloat16)
    share_b = jnp.einsum(
        "bs,brc->src", gather_slots, block_grad_b, precision=lax.Precision.HIGHEST
    ).astype(jnp.bfloat16)
    send_a = (
        jnp.zeros((capacity, adapter_rank_size, width_loc), jnp.bfloat16).at[position].set(share_a)
    )
    send_b = (
        jnp.zeros((capacity, adapter_rank_size, output_location), jnp.bfloat16)
        .at[position]
        .set(share_b)
    )
    back_a, back_b = (
        lax.all_to_all(send_a, "dp", split_axis=0, concat_axis=0, tiled=True),
        lax.all_to_all(send_b, "dp", split_axis=0, concat_axis=0, tiled=True),
    )
    grad_a = jnp.einsum(
        "qk,qrd->krd", serve_adapters, back_a, preferred_element_type=jnp.float32
    ).astype(jnp.bfloat16)
    grad_b = jnp.einsum(
        "qk,qrc->krc", serve_adapters, back_b, preferred_element_type=jnp.float32
    ).astype(jnp.bfloat16)
    return (values, token_gradient, grad_a, grad_b)


def solution(mesh):
    in_specs = (
        P("dp", "mp"),
        P("mp", None),
        P("dp", None, "mp"),
        P("dp", None, "mp"),
        P("dp", "mp"),
        P("dp"),
        P("dp"),
        P(),
    )
    out_specs = (P("dp", "mp"), P("dp", "mp"), P("dp", None, "mp"), P("dp", None, "mp"))
    return jax.shard_map(shards, mesh=mesh, in_specs=in_specs, out_specs=out_specs, check_vma=False)
```

profile of v0, /device:TPU:127, one launch (start us, length us, event | category | flops | bytes accessed | tf_op | source)
XLA Modules:
  0.0 603.8 jit_solution(13908184175450942226)
XLA Ops:
  7.2 1.0 select_reduce_fusion.3
  8.4 0.7 scatter_custom_fusion
  9.1 0.7 all_to_all.18
  9.8 9.6 %all-to-all-start = ((s32[32,2,1]{1,2,0:T(1,128)}), s32[32,2,1]{1,2,0:T(1,128)S(1)}, u32[]{:S(2)}, u32[]{:S(2)}) async-start(s32[32,2,1]{1,2,0:T(1,128)} %bitcast.5), calls=%async_computation.1 | async-start | bytes 32768 | tf_op jit(solution)/shard_map/all_to_all | solution.py:52
  19.5 4.4 all-to-all-done
  23.9 0.5 broadcast.150
  24.4 0.7 reduce.3
  25.2 1.4 convolution_convert_fusion.1
  26.5 1.6 copy.51
  28.2 8.7 %all-to-all-start.2 = ((bf16[64,64,128]{2,1,0:T(8,128)(2,1)}), bf16[64,64,128]{2,1,0:T(8,128)(2,1)}, u32[]{:S(2)}, u32[]{:S(2)}) async-start(bf16[64,64,128]{2,1,0:T(8,128)(2,1)} %copy.51), calls=%async_computation.3 | async-start | bytes 2097152 | tf_op jit(solution)/shard_map/all_to_all | solution.py:64
  36.9 5.7 convolution_convert_fusion
  42.6 11.3 %copy.49 = bf16[64,64,1024]{2,1,0:T(8,128)(2,1)} copy(bf16[64,64,1024]{2,0,1:T(8,128)(2,1)} %convolution_convert_fusion) | data formatting | bytes 16777216 | tf_op jit(solution)/shard_map/convert_element_type | solution.py:58
  53.9 7.4 %all-to-all-done.2 = bf16[64,64,128]{2,1,0:T(8,128)(2,1)} async-done(((bf16[64,64,128]{2,1,0:T(8,128)(2,1)}), bf16[64,64,128]{2,1,0:T(8,128)(2,1)}, u32[]{:S(2)}, u32[]{:S(2)}) %all-to-all-start.2) | async-done | bytes 1048608 | tf_op jit(solution)/shard_map/all_to_all | solution.py:64
  61.3 19.3 %all-to-all-start.1 = ((bf16[64,64,1024]{2,1,0:T(8,128)(2,1)}), bf16[64,64,1024]{2,1,0:T(8,128)(2,1)}, u32[]{:S(2)}, u32[]{:S(2)}) async-start(bf16[64,64,1024]{2,1,0:T(8,128)(2,1)} %copy.49), calls=%async_computation.2 | async-start | bytes 16777216 | tf_op jit(solution)/shard_map/all_to_all | solution.py:63
  81.0 1.9 gather_fusion.2
  82.9 0.6 gather_fusion.3
  83.5 0.4 convolution_bitcast_fusion
  83.9 184.2 %all-to-all-done.1 = bf16[64,64,1024]{2,1,0:T(8,128)(2,1)} async-done(((bf16[64,64,1024]{2,1,0:T(8,128)(2,1)}), bf16[64,64,1024]{2,1,0:T(8,128)(2,1)}, u32[]{:S(2)}, u32[]{:S(2)}) %all-to-all-start.1) | async-done | bytes 8388640 | tf_op jit(solution)/shard_map/all_to_all | solution.py:63
  268.1 6.2 %gather_fusion = bf16[32,64,1024]{2,1,0:T(8,128)(2,1)} fusion(bf16[64,64,1024]{2,1,0:T(8,128)(2,1)} %all-to-all-done.1, s32[1024]{0:T(1024)S(1)} %pad_clamp_fusion.1), kind=kCustom, calls=%fused_computation | custom fusion | bytes 8388736 | tf_op jit(solution)/shard_map/gather | solution.py:66
  274.3 4.9 gather_fusion.1
  279.2 4.2 convolution_bitcast_fusion.1
  283.4 52.8 %all-reduce.2 = (bf16[32,32,64]{2,1,0:T(8,128)(2,1)}, bf16[32,32,64]{2,1,0:T(8,128)(2,1)}) all-reduce(f32[32,32,64]{2,1,0:T(8,128)} %convolution_bitcast_fusion.1, f32[32,32,64]{2,1,0:T(8,128)S(1)} %convolution_bitcast_fusion), channel_id=1, replica_groups=mesh['dp'=32,'mp'=8] {'mp'}, use_global_device_ids=true, to_apply=%region_4.5 | all-reduce | flops 131072 | bytes 786432 | tf_op jit(solution)/shard_map/psum | solution.py:84
  336.3 1.3 fusion.55
  337.6 1.3 convolution_convert_fusion.2
  339.1 1.2 broadcast_in_dim.80
  340.3 4.4 scatter_fusion.1
  344.7 6.9 %all-to-all-start.4 = ((bf16[64,64,128]{2,1,0:T(8,128)(2,1)}), bf16[64,64,128]{2,1,0:T(8,128)(2,1)}, u32[]{:S(2)}, u32[]{:S(2)}) async-start(bf16[64,64,128]{2,1,0:T(8,128)(2,1)} %scatter_fusion.1), calls=%async_computation.5 | async-start | bytes 2097152 | tf_op jit(solution)/shard_map/all_to_all | solution.py:127
  351.6 1.3 fusion.53
  352.8 7.6 %fusion.5 = bf16[32,64,1024]{2,0,1:T(8,128)(2,1)S(1)} fusion(f32[32,64,1024]{2,1,0:T(8,128)S(1)} %fusion.53, s32[32]{0:T(128)S(1)} %select_reduce_fusion), kind=kOutput, calls=%fused_computation.14 | convolution fusion | flops 807404544 | bytes 12583040 | tf_op jit(solution)/shard_map/bs,brd->srd/dot_general | solution.py:111
  360.5 4.2 copy.54
  364.7 4.3 broadcast_in_dim.77
  369.0 11.3 %scatter_fusion = bf16[64,64,1024]{2,1,0:T(8,128)(2,1)} fusion(bf16[64,64,1024]{2,1,0:T(8,128)(2,1)} %broadcast_in_dim.77, s32[32]{0:T(128)S(1)} %fusion.49, bf16[32,64,1024]{2,1,0:T(8,128)(2,1)} %copy.54), kind=kCustom, calls=%fused_computation.5 | custom fusion | bytes 12583040 | tf_op jit(solution)/shard_map/scatter | solution.py:118
  380.4 9.3 %all-to-all-start.3 = ((bf16[64,64,1024]{2,1,0:T(8,128)(2,1)}), bf16[64,64,1024]{2,1,0:T(8,128)(2,1)}, u32[]{:S(2)}, u32[]{:S(2)}) async-start(bf16[64,64,1024]{2,1,0:T(8,128)(2,1)} %scatter_fusion), calls=%async_computation.4 | async-start | bytes 16777216 | tf_op jit(solution)/shard_map/all_to_all | solution.py:126
  389.7 5.9 fusion.52
  395.7 0.2 all-gather.2.cloned.1.call-start
  395.9 0.5 all-gather.2.cloned.1.call-update
  396.6 0.3 fusion.56
  397.1 39.0 %reduce-scatter.2.cloned.1.call-done = f32[128,1024]{1,0:T(8,128)} async-done(((f32[1024,1024]{1,0:T(8,128)}), f32[128,1024]{1,0:T(8,128)}) %reduce-scatter.2.cloned.1.call-update) | async-done | bytes 524304 | tf_op jit(solution)/shard_map/reduce_scatter | solution.py:69
  436.1 1.1 fusion.13
  437.2 0.8 copy.59
  438.0 4.9 fusion.54
  443.0 25.0 %all-gather.2.cloned.1.call-done = bf16[1024,1024]{1,0:T(8,128)(2,1)} async-done(((bf16[1024,128]{1,0:T(8,128)(2,1)}), bf16[1024,1024]{1,0:T(8,128)(2,1)}) %all-gather.2.cloned.1.call-update) | async-done | bytes 2097168 | tf_op jit(solution)/shard_map/all_gather | solution.py:95
  468.0 7.2 %fusion.4 = bf16[1024,1024]{1,0:T(8,128)(2,1)} fusion(f32[32,32,1024]{2,1,0:T(8,128)} %fusion.54, bf16[1024,1024]{1,0:T(8,128)(2,1)} %all-gather.2.cloned.1.call-done, bf16[1024,1024]{1,0:T(8,128)(2,1)} %param.9), kind=kOutput, calls=%fused_computation.13 | convolution fusion | flops 2149580800 | bytes 10485760 | tf_op jit(solution)/shard_map/dot_general | solution.py:94
  475.1 1.9 convolution_convert_fusion.3
  477.0 0.6 copy.61
  477.6 105.8 %all-to-all-done.3 = bf16[64,64,1024]{2,1,0:T(8,128)(2,1)} async-done(((bf16[64,64,1024]{2,1,0:T(8,128)(2,1)}), bf16[64,64,1024]{2,1,0:T(8,128)(2,1)}, u32[]{:S(2)}, u32[]{:S(2)}) %all-to-all-start.3) | async-done | bytes 8388640 | tf_op jit(solution)/shard_map/all_to_all | solution.py:126
  583.4 12.3 %fusion.8 = bf16[3,64,1024]{2,0,1:T(4,128)(2,1)S(1)} fusion(bf16[64,64,1024]{2,1,0:T(8,128)(2,1)} %all-to-all-done.3, s32[64]{0:T(128)S(1)} %eq.42, s32[3]{0:T(128)S(1)} %iota_add_fusion), kind=kOutput, calls=%fused_computation.16 | convolution fusion | flops 25362624 | bytes 8782092 | tf_op jit(solution)/shard_map/qk,qrd->krd/dot_general | solution.py:129
  595.7 0.9 copy.60
  (29 shorter events, 1.4 us)
Async XLA Ops:
  7.2 272.1 %copy-start = (bf16[1024,1024]{1,0:T(8,128)(2,1)S(1)}, bf16[1024,1024]{1,0:T(8,128)(2,1)}, u32[]{:S(2)}) copy-start(bf16[1024,1024]{1,0:T(8,128)(2,1)} %param.8) | copy-start | bytes 6291460
  7.2 29.7 %copy-start.4 = (bf16[3,64,1024]{2,1,0:T(8,128)(2,1)S(1)}, bf16[3,64,1024]{2,1,0:T(8,128)(2,1)}, u32[]{:S(2)}) copy-start(bf16[3,64,1024]{2,1,0:T(8,128)(2,1)} %param.10) | copy-start | bytes 1179652
  9.8 14.0 %all-to-all-start = ((s32[32,2,1]{1,2,0:T(1,128)}), s32[32,2,1]{1,2,0:T(1,128)S(1)}, u32[]{:S(2)}, u32[]{:S(2)}) async-start(s32[32,2,1]{1,2,0:T(1,128)} %bitcast.5), calls=%async_computation.1 | async-start | bytes 32768 | tf_op jit(solution)/shard_map/all_to_all | solution.py:52
  28.2 33.1 %all-to-all-start.2 = ((bf16[64,64,128]{2,1,0:T(8,128)(2,1)}), bf16[64,64,128]{2,1,0:T(8,128)(2,1)}, u32[]{:S(2)}, u32[]{:S(2)}) async-start(bf16[64,64,128]{2,1,0:T(8,128)(2,1)} %copy.51), calls=%async_computation.3 | async-start | bytes 2097152 | tf_op jit(solution)/shard_map/all_to_all | solution.py:64
  53.9 26.7 %copy-start.6 = (s32[32]{0:T(128)S(1)}, s32[32]{0:T(128)}, u32[]{:S(2)}) copy-start(s32[32]{0:T(128)} %param.13) | copy-start | bytes 388
  53.9 26.7 %copy-start.5 = (s32[32]{0:T(128)S(1)}, s32[32]{0:T(128)}, u32[]{:S(2)}) copy-start(s32[32]{0:T(128)} %param.14) | copy-start | bytes 388
  53.9 29.7 %copy-start.1 = (bf16[1024,128]{1,0:T(8,128)(2,1)S(1)}, bf16[1024,128]{1,0:T(8,128)(2,1)}, u32[]{:S(2)}) copy-start(bf16[1024,128]{1,0:T(8,128)(2,1)} %param.12) | copy-start | bytes 786436
  61.3 206.8 %all-to-all-start.1 = ((bf16[64,64,1024]{2,1,0:T(8,128)(2,1)}), bf16[64,64,1024]{2,1,0:T(8,128)(2,1)}, u32[]{:S(2)}, u32[]{:S(2)}) async-start(bf16[64,64,1024]{2,1,0:T(8,128)(2,1)} %copy.49), calls=%async_computation.2 | async-start | bytes 16777216 | tf_op jit(solution)/shard_map/all_to_all | solution.py:63
  336.3 15.3 %copy-start.3 = (bf16[32,32,64]{2,1,0:T(8,128)(2,1)S(1)}, bf16[32,32,64]{2,1,0:T(8,128)(2,1)}, u32[]{:S(2)}) copy-start(bf16[32,32,64]{2,1,0:T(8,128)(2,1)} %get-tuple-element.21) | copy-start | bytes 393220
  344.7 35.7 %all-to-all-start.4 = ((bf16[64,64,128]{2,1,0:T(8,128)(2,1)}), bf16[64,64,128]{2,1,0:T(8,128)(2,1)}, u32[]{:S(2)}, u32[]{:S(2)}) async-start(bf16[64,64,128]{2,1,0:T(8,128)(2,1)} %scatter_fusion.1), calls=%async_computation.5 | async-start | bytes 2097152 | tf_op jit(solution)/shard_map/all_to_all | solution.py:127
  380.4 203.1 %all-to-all-start.3 = ((bf16[64,64,1024]{2,1,0:T(8,128)(2,1)}), bf16[64,64,1024]{2,1,0:T(8,128)(2,1)}, u32[]{:S(2)}, u32[]{:S(2)}) async-start(bf16[64,64,1024]{2,1,0:T(8,128)(2,1)} %scatter_fusion), calls=%async_computation.4 | async-start | bytes 16777216 | tf_op jit(solution)/shard_map/all_to_all | solution.py:126
  389.6 46.4 %reduce-scatter.2.cloned.1.call-start = ((), (), s32[]{:S(2)}) async-start(), calls=%async_computation.6 | async-start | bytes 4718592 | tf_op jit(solution)/shard_map/reduce_scatter | solution.py:69
  395.6 0.9 copy-start.2
  395.7 72.3 %all-gather.2.cloned.1.call-start = ((), (), s32[]{:S(2)}) async-start(), calls=%async_computation.7 | async-start | bytes 2359296 | tf_op jit(solution)/shard_map/all_gather | solution.py:95
Sparse Core Ops, SparseCore 0:
  395.8 40.2 reduce-scatter.1
  437.9 30.0 all-gather.1
where the time goes:
time: 613 us; the launch traced here: 604 us
  waiting for transfers between devices  366 us (60%)
  local copies, waits for them, and re-layouts  57 us (9%)
  matrix products  55.7 us (9%)
  starting transfers between devices  54 us (9%)
  blocking collectives  52.8 us (9%)
  between operations  14.7 us (2%)
    all_to_all x1, waiting for transfers between devices, shards(): lax.all_to_all(returned_down_panel, 'dp', split_axis=0, concat_axis=0, ti...  184 us
    all_to_all x1, waiting for transfers between devices, shards(): lax.all_to_all(send_a, 'dp', split_axis=0, concat_axis=0, tiled=True)  106 us
    psum x1, blocking collectives, shards(): down_low = lax.psum(down_part, 'mp').astype(jnp.bfloat16)  52.8 us
    reduce_scatter x1, waiting for transfers between devices, shards(): lax.psum_scatter(lax.dot_general(w_cols, tokens, (((0,), (1,)), ((), ()))...  39 us
    all_gather x1, waiting for transfers between devices, shards(): lax.all_gather(cotangent, 'mp', axis=1, tiled=True)  25 us
    all_to_all x1, starting transfers between devices, shards(): lax.all_to_all(returned_down_panel, 'dp', split_axis=0, concat_axis=0, ti...  19.3 us
    dot_general x1, matrix products, shards(): jnp.einsum('qk,qrd->krd', serve_adapters, back_a, preferred_element_type=...  12.3 us
  transfers between devices with their start and end apart: 7, of which 6 were waited for; matrix products, arithmetic and copies ran while one was open for 12% of the time, Pallas kernels for 0%

commit v1 on v0

--- a/solution.py
+++ b/solution.py
@@ -81,7 +81,7 @@
     down_part = jnp.einsum(
         "bnd,brd->bnr", token_blocks, block_down_panel, preferred_element_type=jnp.float32
     )
-    down_low = lax.psum(down_part, "mp").astype(jnp.bfloat16)
+    down_low = jnp.sum(lax.all_gather(down_part, "mp"), axis=0).astype(jnp.bfloat16)
     adapter_output = jnp.einsum(
         "afq,aqy->afy", down_low, block_up_panel, preferred_element_type=jnp.float32
     ).reshape(rows, output_location)

time: 613 us -> 509 us (0.83)
  the two profiles are of different devices: /device:TPU:127 before, /device:TPU:18 now
where the time goes in v1:
time: 509 us; the launch traced here: 500 us
  waiting for transfers between devices  282 us (55%)
  local copies, waits for them, and re-layouts  60.1 us (12%)
  matrix products  55.3 us (11%)
  starting transfers between devices  43.9 us (9%)
  blocking collectives  38 us (7%)
  between operations  14.4 us (3%)
  other arithmetic  6.19 us (1%)
    all_to_all x1, waiting for transfers between devices, shards(): lax.all_to_all(send_a, 'dp', split_axis=0, concat_axis=0, tiled=True)  126 us
    all_to_all x1, waiting for transfers between devices, shards(): lax.all_to_all(returned_down_panel, 'dp', split_axis=0, concat_axis=0, ti...  109 us
    psum x1, blocking collectives, shards(): up_grad = lax.psum(up_part, 'mp').astype(jnp.bfloat16)  38 us
    all_gather x1, waiting for transfers between devices, shards(): lax.all_gather(down_part, 'mp')  27.7 us
    all_to_all x1, starting transfers between devices, shards(): lax.all_to_all(send_a, 'dp', split_axis=0, concat_axis=0, tiled=True)  12.6 us
    dot_general x1, matrix products, shards(): jnp.einsum('qk,qrd->krd', serve_adapters, back_a, preferred_element_type=...  12.3 us
    all_to_all x1, starting transfers between devices, shards(): lax.all_to_all(requests, 'dp', split_axis=0, concat_axis=0, tiled=True)  11.6 us
    scatter x1, local copies, waits for them, and re-layouts, shards(): jnp.zeros((capacity, adapter_rank_size, width_loc), jnp.bfloat16)  11.3 us
  transfers between devices with their start and end apart: 8, of which 5 were waited for; matrix products, arithmetic and copies ran while one was open for 22% of the time, Pallas kernels for 0%

profile of v1, /device:TPU:18, one launch (start us, length us, event | category | flops | bytes accessed | tf_op | source)
XLA Modules:
  0.0 499.8 jit_solution(2229507911706907366)
XLA Ops:
  7.2 1.0 select_reduce_fusion.3
  8.4 0.7 scatter_custom_fusion
  9.1 0.7 all_to_all.18
  9.8 11.6 %all-to-all-start = ((s32[32,2,1]{1,2,0:T(1,128)}), s32[32,2,1]{1,2,0:T(1,128)S(1)}, u32[]{:S(2)}, u32[]{:S(2)}) async-start(s32[32,2,1]{1,2,0:T(1,128)} %bitcast.5), calls=%async_computation.1 | async-start | bytes 32768 | tf_op jit(solution)/shard_map/all_to_all | solution.py:52
  21.5 8.4 %all-to-all-done = s32[32,2,1]{1,2,0:T(1,128)S(1)} async-done(((s32[32,2,1]{1,2,0:T(1,128)}), s32[32,2,1]{1,2,0:T(1,128)S(1)}, u32[]{:S(2)}, u32[]{:S(2)}) %all-to-all-start) | async-done | bytes 288 | tf_op jit(solution)/shard_map/all_to_all | solution.py:52
  29.9 0.5 broadcast.150
  30.4 0.7 reduce.3
  31.2 1.4 convolution_convert_fusion.1
  32.6 1.6 copy.51
  34.2 5.7 %all-to-all-start.2 = ((bf16[64,64,128]{2,1,0:T(8,128)(2,1)}), bf16[64,64,128]{2,1,0:T(8,128)(2,1)}, u32[]{:S(2)}, u32[]{:S(2)}) async-start(bf16[64,64,128]{2,1,0:T(8,128)(2,1)} %copy.51), calls=%async_computation.3 | async-start | bytes 2097152 | tf_op jit(solution)/shard_map/all_to_all | solution.py:64
  39.9 5.7 %convolution_convert_fusion = bf16[64,64,1024]{2,0,1:T(8,128)(2,1)} fusion(bf16[3,64,1024]{2,1,0:T(8,128)(2,1)S(1)} %copy-done.3, s32[64]{0:T(128)S(1)} %eq.42, s32[3]{0:T(128)S(1)} %iota_add_fusion), kind=kOutput, calls=%fused_computation.11 | convolution fusion | flops 29360320 | bytes 8782092 | tf_op jit(solution)/shard_map/vj,jiz->viz/dot_general | solution.py:56
  45.6 11.3 %copy.49 = bf16[64,64,1024]{2,1,0:T(8,128)(2,1)} copy(bf16[64,64,1024]{2,0,1:T(8,128)(2,1)} %convolution_convert_fusion) | data formatting | bytes 16777216 | tf_op jit(solution)/shard_map/convert_element_type | solution.py:58
  56.9 10.1 %all-to-all-done.2 = bf16[64,64,128]{2,1,0:T(8,128)(2,1)} async-done(((bf16[64,64,128]{2,1,0:T(8,128)(2,1)}), bf16[64,64,128]{2,1,0:T(8,128)(2,1)}, u32[]{:S(2)}, u32[]{:S(2)}) %all-to-all-start.2) | async-done | bytes 1048608 | tf_op jit(solution)/shard_map/all_to_all | solution.py:64
  67.0 5.6 %all-to-all-start.1 = ((bf16[64,64,1024]{2,1,0:T(8,128)(2,1)}), bf16[64,64,1024]{2,1,0:T(8,128)(2,1)}, u32[]{:S(2)}, u32[]{:S(2)}) async-start(bf16[64,64,1024]{2,1,0:T(8,128)(2,1)} %copy.49), calls=%async_computation.2 | async-start | bytes 16777216 | tf_op jit(solution)/shard_map/all_to_all | solution.py:63
  73.0 2.6 gather_fusion.2
  75.7 1.7 gather_fusion.3
  77.4 1.2 convolution_bitcast_fusion
  78.5 38.0 %all-reduce.1 = bf16[32,32,64]{2,1,0:T(8,128)(2,1)S(1)} all-reduce(f32[32,32,64]{2,1,0:T(8,128)} %convolution_bitcast_fusion), channel_id=1, replica_groups=mesh['dp'=32,'mp'=8] {'mp'}, use_global_device_ids=true, to_apply=%region_5.6 | all-reduce | flops 65536 | bytes 393216 | tf_op jit(solution)/shard_map/psum | solution.py:92
  116.6 1.3 fusion.53
  117.9 7.6 %fusion.5 = bf16[32,64,1024]{2,0,1:T(8,128)(2,1)S(1)} fusion(f32[32,64,1024]{2,1,0:T(8,128)S(1)} %fusion.53, s32[32]{0:T(128)S(1)} %select_reduce_fusion), kind=kOutput, calls=%fused_computation.14 | convolution fusion | flops 807404544 | bytes 12583040 | tf_op jit(solution)/shard_map/bs,brd->srd/dot_general | solution.py:111
  125.5 4.3 copy.54
  129.8 4.3 broadcast_in_dim.77
  134.1 11.3 %scatter_fusion = bf16[64,64,1024]{2,1,0:T(8,128)(2,1)} fusion(bf16[64,64,1024]{2,1,0:T(8,128)(2,1)} %broadcast_in_dim.77, s32[32]{0:T(128)S(1)} %fusion.49, bf16[32,64,1024]{2,1,0:T(8,128)(2,1)} %copy.54), kind=kCustom, calls=%fused_computation.5 | custom fusion | bytes 12583040 | tf_op jit(solution)/shard_map/scatter | solution.py:118
  145.5 108.6 %all-to-all-done.1 = bf16[64,64,1024]{2,1,0:T(8,128)(2,1)} async-done(((bf16[64,64,1024]{2,1,0:T(8,128)(2,1)}), bf16[64,64,1024]{2,1,0:T(8,128)(2,1)}, u32[]{:S(2)}, u32[]{:S(2)}) %all-to-all-start.1) | async-done | bytes 8388640 | tf_op jit(solution)/shard_map/all_to_all | solution.py:63
  254.1 12.6 %all-to-all-start.3 = ((bf16[64,64,1024]{2,1,0:T(8,128)(2,1)}), bf16[64,64,1024]{2,1,0:T(8,128)(2,1)}, u32[]{:S(2)}, u32[]{:S(2)}) async-start(bf16[64,64,1024]{2,1,0:T(8,128)(2,1)} %scatter_fusion), calls=%async_computation.4 | async-start | bytes 16777216 | tf_op jit(solution)/shard_map/all_to_all | solution.py:126
  266.8 6.2 %gather_fusion = bf16[32,64,1024]{2,1,0:T(8,128)(2,1)} fusion(bf16[64,64,1024]{2,1,0:T(8,128)(2,1)} %all-to-all-done.1, s32[1024]{0:T(1024)S(1)} %pad_clamp_fusion.1), kind=kCustom, calls=%fused_computation | custom fusion | bytes 8388736 | tf_op jit(solution)/shard_map/gather | solution.py:66
  273.0 5.0 gather_fusion.1
  277.9 4.2 convolution_bitcast_fusion.1
  282.2 0.7 all-gather.4.cloned.1.call-update
  283.0 5.9 %fusion.52 = f32[1024,1024]{1,0:T(8,128)} fusion(bf16[1024,1024]{1,0:T(8,128)(2,1)} %param.9, bf16[1024,1024]{1,0:T(8,128)(2,1)S(1)} %copy-done), kind=kOutput, calls=%fused_computation.79 | convolution fusion | flops 2147483648 | bytes 8388608 | tf_op jit(solution)/shard_map/dot_general | solution.py:70
  288.9 27.7 %all-gather.6.cloned.1.call-done = f32[256,32,64]{2,1,0:T(8,128)} async-done(((f32[32,32,64]{2,1,0:T(8,128)}), f32[256,32,64]{2,1,0:T(8,128)}) %all-gather.6.cloned.1.call-update) | async-done | bytes 2097168 | tf_op jit(solution)/shard_map/all_gather | solution.py:84
  316.6 2.8 reduce_sum.41
  319.4 0.3 fusion.55
  319.8 1.3 convolution_convert_fusion.2
  321.1 1.0 copy.57
  322.1 1.3 broadcast_in_dim.80
  323.4 4.8 scatter_fusion.1
  328.2 126.4 %all-to-all-done.3 = bf16[64,64,1024]{2,1,0:T(8,128)(2,1)} async-done(((bf16[64,64,1024]{2,1,0:T(8,128)(2,1)}), bf16[64,64,1024]{2,1,0:T(8,128)(2,1)}, u32[]{:S(2)}, u32[]{:S(2)}) %all-to-all-start.3) | async-done | bytes 8388640 | tf_op jit(solution)/shard_map/all_to_all | solution.py:126
  454.5 8.2 %all-to-all-start.4 = ((bf16[64,64,128]{2,1,0:T(8,128)(2,1)}), bf16[64,64,128]{2,1,0:T(8,128)(2,1)}, u32[]{:S(2)}, u32[]{:S(2)}) async-start(bf16[64,64,128]{2,1,0:T(8,128)(2,1)} %scatter_fusion.1), calls=%async_computation.5 | async-start | bytes 2097152 | tf_op jit(solution)/shard_map/all_to_all | solution.py:127
  462.7 4.8 fusion.54
  467.5 7.2 %fusion.4 = bf16[1024,1024]{1,0:T(8,128)(2,1)} fusion(f32[32,32,1024]{2,1,0:T(8,128)} %fusion.54, bf16[1024,1024]{1,0:T(8,128)(2,1)} %all-gather.4.cloned.1.call-done, bf16[1024,1024]{1,0:T(8,128)(2,1)} %param.9), kind=kOutput, calls=%fused_computation.13 | convolution fusion | flops 2149580800 | bytes 10485760 | tf_op jit(solution)/shard_map/dot_general | solution.py:94
  474.7 12.3 %fusion.8 = bf16[3,64,1024]{2,0,1:T(4,128)(2,1)S(1)} fusion(bf16[64,64,1024]{2,1,0:T(8,128)(2,1)} %all-to-all-done.3, s32[64]{0:T(128)S(1)} %eq.42, s32[3]{0:T(128)S(1)} %iota_add_fusion), kind=kOutput, calls=%fused_computation.16 | convolution fusion | flops 25362624 | bytes 8782092 | tf_op jit(solution)/shard_map/qk,qrd->krd/dot_general | solution.py:129
  487.0 0.9 copy.60
  487.9 0.3 fusion.56
  488.4 1.1 fusion.13
  489.5 0.8 copy.59
  490.3 1.9 convolution_convert_fusion.3
  492.2 0.6 copy.61
  (31 shorter events, 1.1 us)
Async XLA Ops:
  7.2 109.4 %copy-start = (bf16[1024,1024]{1,0:T(8,128)(2,1)S(1)}, bf16[1024,1024]{1,0:T(8,128)(2,1)}, u32[]{:S(2)}) copy-start(bf16[1024,1024]{1,0:T(8,128)(2,1)} %param.8) | copy-start | bytes 6291460
  7.2 32.7 %copy-start.3 = (bf16[3,64,1024]{2,1,0:T(8,128)(2,1)S(1)}, bf16[3,64,1024]{2,1,0:T(8,128)(2,1)}, u32[]{:S(2)}) copy-start(bf16[3,64,1024]{2,1,0:T(8,128)(2,1)} %param.10) | copy-start | bytes 1179652
  9.8 20.1 %all-to-all-start = ((s32[32,2,1]{1,2,0:T(1,128)}), s32[32,2,1]{1,2,0:T(1,128)S(1)}, u32[]{:S(2)}, u32[]{:S(2)}) async-start(s32[32,2,1]{1,2,0:T(1,128)} %bitcast.5), calls=%async_computation.1 | async-start | bytes 32768 | tf_op jit(solution)/shard_map/all_to_all | solution.py:52
  34.2 32.7 %all-to-all-start.2 = ((bf16[64,64,128]{2,1,0:T(8,128)(2,1)}), bf16[64,64,128]{2,1,0:T(8,128)(2,1)}, u32[]{:S(2)}, u32[]{:S(2)}) async-start(bf16[64,64,128]{2,1,0:T(8,128)(2,1)} %copy.51), calls=%async_computation.3 | async-start | bytes 2097152 | tf_op jit(solution)/shard_map/all_to_all | solution.py:64
  56.9 15.7 %copy-start.5 = (s32[32]{0:T(128)S(1)}, s32[32]{0:T(128)}, u32[]{:S(2)}) copy-start(s32[32]{0:T(128)} %param.13) | copy-start | bytes 388
  56.9 15.7 %copy-start.4 = (s32[32]{0:T(128)S(1)}, s32[32]{0:T(128)}, u32[]{:S(2)}) copy-start(s32[32]{0:T(128)} %param.14) | copy-start | bytes 388
  56.9 20.4 %copy-start.1 = (bf16[1024,128]{1,0:T(8,128)(2,1)S(1)}, bf16[1024,128]{1,0:T(8,128)(2,1)}, u32[]{:S(2)}) copy-start(bf16[1024,128]{1,0:T(8,128)(2,1)} %param.12) | copy-start | bytes 786436
  67.0 187.1 %all-to-all-start.1 = ((bf16[64,64,1024]{2,1,0:T(8,128)(2,1)}), bf16[64,64,1024]{2,1,0:T(8,128)(2,1)}, u32[]{:S(2)}, u32[]{:S(2)}) async-start(bf16[64,64,1024]{2,1,0:T(8,128)(2,1)} %copy.49), calls=%async_computation.2 | async-start | bytes 16777216 | tf_op jit(solution)/shard_map/all_to_all | solution.py:63
  254.1 200.4 %all-to-all-start.3 = ((bf16[64,64,1024]{2,1,0:T(8,128)(2,1)}), bf16[64,64,1024]{2,1,0:T(8,128)(2,1)}, u32[]{:S(2)}, u32[]{:S(2)}) async-start(bf16[64,64,1024]{2,1,0:T(8,128)(2,1)} %scatter_fusion), calls=%async_computation.4 | async-start | bytes 16777216 | tf_op jit(solution)/shard_map/all_to_all | solution.py:126
  266.7 49.9 %all-gather.6.cloned.1.call-start = ((), (), s32[]{:S(2)}) async-start(), calls=%async_computation.8 | async-start | bytes 4718592 | tf_op jit(solution)/shard_map/all_gather | solution.py:84
  282.2 185.4 %all-gather.4.cloned.1.call-start = ((), (), s32[]{:S(2)}) async-start(), calls=%async_computation.7 | async-start | bytes 2359296 | tf_op jit(solution)/shard_map/all_gather | solution.py:95
  282.9 205.5 %reduce-scatter.2.cloned.1.call-start = ((), (), s32[]{:S(2)}) async-start(), calls=%async_computation.6 | async-start | bytes 4718592 | tf_op jit(solution)/shard_map/reduce_scatter | solution.py:69
  288.9 30.5 %copy-start.2 = (bf16[1024,128]{1,0:T(8,128)(2,1)S(1)}, bf16[1024,128]{1,0:T(8,128)(2,1)}, u32[]{:S(2)}) copy-start(bf16[1024,128]{1,0:T(8,128)(2,1)} %param.12) | copy-start | bytes 786436
  454.5 35.8 %all-to-all-start.4 = ((bf16[64,64,128]{2,1,0:T(8,128)(2,1)}), bf16[64,64,128]{2,1,0:T(8,128)(2,1)}, u32[]{:S(2)}, u32[]{:S(2)}) async-start(bf16[64,64,128]{2,1,0:T(8,128)(2,1)} %scatter_fusion.1), calls=%async_computation.5 | async-start | bytes 2097152 | tf_op jit(solution)/shard_map/all_to_all | solution.py:127
Sparse Core Ops, SparseCore 0:
  282.3 34.2 all-gather.5
  318.4 30.8 all-gather.3
  351.8 37.1 reduce-scatter.1
